TPU v7x, 128 devices: a whole 4x4x4 slice. The times are simulated.
128 devices in a mesh: req: 16 (over y, x), head: 8 (over z, core).
Axes of the slice: x: 4, y: 4, z: 4, core: 2. Of those that a mesh axis runs over, the one named last changes fastest.
Arguments:
- hidden_in: bfloat16 [8192, 2048], P(('req', 'head')), may hold values from -6 to 6
- segment_ids: int32 [16, 512], P('req', 'head'), may hold values from 0 to 3, never falling along the last dimension, each value on 1 to 256 neighbouring positions
- attn_routes: int32 [8192, 2], P(('req', 'head')), may hold values from 0 to 7, all different within a row; in each aligned block of 512 rows (0 to 511, 512 to 1023, ...) at most 192 rows name the same one
- ffn_routes: int32 [8192, 2], P(('req', 'head')), may hold values from 0 to 7, all different within a row; in each aligned block of 64 rows (0 to 63, 64 to 127, ...) at most 24 rows name the same one
- attn_gain: float32 [2048], replicated, may hold values from 0.1 to 1.9
- attn_router: float32 [2048, 8], replicated, may hold values from -0.125 to 0.125
- w_query: bfloat16 [8, 2048, 2048], P(None, None, 'head'), may hold values from -1 to 1
- w_key: bfloat16 [2048, 2048], P(None, 'head'), may hold values from -32 to 32
- w_value: bfloat16 [2048, 2048], P(None, 'head'), may hold values from -0.125 to 0.125
- w_out: bfloat16 [8, 2048, 2048], P(None, 'head'), may hold values from -0.125 to 0.125
- ffn_gain: float32 [2048], replicated, may hold values from 0.1 to 1.9
- ffn_router: float32 [2048, 8], replicated, may hold values from -0.125 to 0.125
- w_gate_up: bfloat16 [8, 2048, 2, 5632], P('head', None, None, 'req'), may hold values from -0.125 to 0.125
- w_down: bfloat16 [8, 5632, 2048], P('head', 'req'), may hold values from -0.078125 to 0.078125
Outputs:
- layer_out: bfloat16 [8192, 2048], P(('req', 'head'))
Inputs may be any that keep to these rules, and one draw needn't show every extreme that they name: `segment_ids`: within each row segment numbers never fall; each segment has 1 to 256 tokens. `attn_routes`: each token names two different experts; in each aligned block of 512 rows no expert is named by more than 192 rows. `ffn_routes`: each token names two different experts; in each aligned block of 64 rows (the rows of one device) no expert is named by more than 24 rows.
All inputs are finite; a program needn't handle non-finite values.
Results may differ from a plain program's by a relative error of at most 0.015.
Values may be sent and summed in bfloat16 or wider, within the bound.
No kernel may reach another device: no remote copies, remote signals or barrier semaphores. Data moves between devices by JAX's collectives and lax.ppermute only.
A program may use at most 128 MiB of HBM per device.

v0:
```python
import jax
import jax.numpy as jnp
from jax import lax
from jax.sharding import PartitionSpec as P

D = 2048
HD = 128
E_ATT = 8
E_FF = 8
EPSILON = 1e-06
ROPE_BASE = 10000.0


def rms_norm(values, gain_vector):
    widened = values.astype(jnp.float32)
    inverse_rms = lax.rsqrt(jnp.mean(widened * widened, axis=-1, keepdims=True) + EPSILON)
    return (widened * inverse_rms * gain_vector).astype(jnp.bfloat16)


def pair_gates(normed, router, routes):
    logits = jnp.dot(normed.astype(jnp.float32), router, precision=lax.Precision.HIGHEST)
    picked = jnp.take_along_axis(logits, routes, axis=1)
    first_weight = jax.nn.sigmoid(picked[:, 0] - picked[:, 1])
    second_weight = jax.nn.sigmoid(picked[:, 1] - picked[:, 0])
    return jnp.stack([first_weight, second_weight], axis=1)


def positions(segment_row):
    earlier = (segment_row[None, :] < segment_row[:, None]).astype(jnp.int32)
    return jnp.arange(segment_row.shape[0], dtype=jnp.int32) - jnp.sum(earlier, axis=1)


def rotary(values, token_place):
    half_width = values.shape[-1] // 2
    inverse = ROPE_BASE ** (-jnp.arange(half_width, dtype=jnp.float32) / half_width)
    shaped = token_place.astype(jnp.float32).reshape((-1,) + (1,) * (values.ndim - 2) + (1,))
    angles = shaped * inverse
    cosine = jnp.cos(angles)
    sines = jnp.sin(angles)
    lower_half = values[..., :half_width]
    upper_half = values[..., half_width:]
    return jnp.concatenate(
        [lower_half * cosine - upper_half * sines, upper_half * cosine + lower_half * sines],
        axis=-1,
    )


def slot_ranks(experts_flat, expert_count):
    onehot = (experts_flat[:, None] == jnp.arange(expert_count, dtype=jnp.int32)[None, :]).astype(
        jnp.int32
    )
    running = jnp.cumsum(onehot, axis=0) - onehot
    return jnp.sum(running * onehot, axis=1)


def soft_weights(scores, allowed):
    masked = jnp.where(allowed, scores, -1e30)
    largest = jnp.max(masked, axis=-1, keepdims=True)
    exponent = jnp.exp(masked - largest)
    return (exponent / jnp.sum(exponent, axis=-1, keepdims=True)).astype(jnp.bfloat16)


def per_device(
    hidden_in,
    segment_ids,
    attn_routes,
    ffn_routes,
    attn_gain,
    attn_router,
    w_query,
    w_key,
    w_value,
    w_out,
    ffn_gain,
    ffn_router,
    w_gate_up,
    w_down,
):
    row_count = hidden_in.shape[0]
    head_count = lax.axis_size("head")
    seq_length = row_count * head_count
    capacity = 3 * seq_length // 8
    local_width = w_key.shape[1]
    local_heads = local_width // HD
    normed = rms_norm(hidden_in, attn_gain)
    normed_all, segment_all, routes_all = (
        lax.all_gather(normed, "head", axis=0, tiled=True),
        lax.all_gather(segment_ids, "head", axis=1, tiled=True),
        lax.all_gather(attn_routes, "head", axis=0, tiled=True),
    )
    segment_row = segment_all[0]
    token_place = positions(segment_row)
    pair_weights = pair_gates(normed_all, attn_router, routes_all)
    flat_experts = routes_all.reshape(-1)
    slot_index = flat_experts * capacity + slot_ranks(flat_experts, E_ATT)
    slot_table = (
        jnp.full((E_ATT * capacity,), 2 * seq_length, jnp.int32)
        .at[slot_index]
        .set(jnp.arange(2 * seq_length, dtype=jnp.int32))
    )
    padded = jnp.concatenate([normed_all, jnp.zeros((1, D), jnp.bfloat16)], axis=0)
    buffer = padded[slot_table // 2].reshape(E_ATT, capacity, D)
    query_buf = jnp.einsum("ecd,edf->ecf", buffer, w_query, preferred_element_type=jnp.float32)
    queries = query_buf.reshape(E_ATT * capacity, local_width)[slot_index].reshape(
        seq_length, 2, local_heads, HD
    )
    queries = rotary(queries, token_place).astype(jnp.bfloat16)
    key_heads = jnp.dot(normed_all, w_key, preferred_element_type=jnp.float32).reshape(
        seq_length, local_heads, HD
    )
    key_heads = rotary(key_heads, token_place).astype(jnp.bfloat16)
    value_heads = (
        jnp.dot(normed_all, w_value, preferred_element_type=jnp.float32)
        .astype(jnp.bfloat16)
        .reshape(seq_length, local_heads, HD)
    )
    block_rows = min(seq_length, 512)
    block_total = seq_length // block_rows
    key_index = jnp.arange(seq_length, dtype=jnp.int32)

    def attend(block_input):
        query_block, offset = block_input
        scores = jnp.einsum(
            "tjgd,sgd->gjts", query_block, key_heads, preferred_element_type=jnp.float32
        ) * HD ** (-0.5)
        query_index = offset + jnp.arange(block_rows, dtype=jnp.int32)
        allowed = (segment_row[:, None] == segment_row[None, :]) & (
            key_index[None, :] <= query_index[:, None]
        )
        probs = soft_weights(scores, allowed)
        return jnp.einsum(
            "gjts,sgd->tjgd", probs, value_heads, preferred_element_type=jnp.float32
        ).astype(jnp.bfloat16)

    contexts = lax.map(
        attend,
        (
            queries.reshape(block_total, block_rows, 2, local_heads, HD),
            jnp.arange(block_total, dtype=jnp.int32) * block_rows,
        ),
    )
    context = contexts.reshape(2 * seq_length, local_width)
    padded_ctx = jnp.concatenate([context, jnp.zeros((1, local_width), jnp.bfloat16)], axis=0)
    out_buf = padded_ctx[slot_table].reshape(E_ATT, capacity, local_width)
    projected = jnp.einsum("ecf,efd->ecd", out_buf, w_out, preferred_element_type=jnp.float32)
    per_pair = (
        projected.reshape(E_ATT * capacity, D)[slot_index] * pair_weights.reshape(-1)[:, None]
    )
    partial_value = jnp.sum(per_pair.reshape(seq_length, 2, D), axis=1)
    attn_rows = lax.psum_scatter(
        partial_value.astype(jnp.bfloat16), "head", scatter_dimension=0, tiled=True
    ).astype(jnp.float32)
    residual = (hidden_in.astype(jnp.float32) + attn_rows).astype(jnp.bfloat16)
    ffn_normed = rms_norm(residual, ffn_gain)
    ffn_weights = pair_gates(ffn_normed, ffn_router, ffn_routes)
    cap_ffn = 3 * row_count // 8
    local_experts = w_gate_up.shape[0]
    experts_flat = ffn_routes.reshape(-1)
    destination = experts_flat * cap_ffn + slot_ranks(experts_flat, E_FF)
    send_table = (
        jnp.full((E_FF * cap_ffn,), 2 * row_count, jnp.int32)
        .at[destination]
        .set(jnp.arange(2 * row_count, dtype=jnp.int32))
    )
    padded_ffn = jnp.concatenate([ffn_normed, jnp.zeros((1, D), jnp.bfloat16)], axis=0)
    outgoing = padded_ffn[send_table // 2].reshape(head_count, local_experts * cap_ffn, D)
    arrived = lax.all_to_all(outgoing, "head", split_axis=0, concat_axis=0, tiled=True)
    shard_rows = lax.all_gather(arrived, "req", axis=0, tiled=True)
    row_total = shard_rows.shape[0]
    grouped = shard_rows.reshape(row_total, local_experts, cap_ffn, D)
    gate_up = jnp.einsum("mecd,edgf->mecgf", grouped, w_gate_up, preferred_element_type=jnp.float32)
    activated = (jax.nn.silu(gate_up[..., 0, :]) * gate_up[..., 1, :]).astype(jnp.bfloat16)
    partials = jnp.einsum(
        "mecf,efd->mecd", activated, w_down, preferred_element_type=jnp.float32
    ).astype(jnp.bfloat16)
    partials = lax.optimization_barrier(partials).astype(jnp.float32)
    summed = lax.psum_scatter(
        partials.reshape(lax.axis_size("req") * head_count, local_experts * cap_ffn, D).astype(
            jnp.bfloat16
        ),
        "req",
        scatter_dimension=0,
        tiled=True,
    )
    returned = lax.all_to_all(summed, "head", split_axis=0, concat_axis=0, tiled=True)
    expert_rows = returned.reshape(-1, D)[destination]
    mixture = jnp.sum(
        expert_rows.astype(jnp.float32).reshape(row_count, 2, D) * ffn_weights[:, :, None], axis=1
    )
    return (residual.astype(jnp.float32) + mixture).astype(jnp.bfloat16)


def solution(mesh):
    return jax.shard_map(
        per_device,
        mesh=mesh,
        in_specs=(
            P(("req", "head"), None),
            P("req", "head"),
            P(("req", "head"), None),
            P(("req", "head"), None),
            P(),
            P(),
            P(None, None, "head"),
            P(None, "head"),
            P(None, "head"),
            P(None, "head", None),
            P(),
            P(),
            P("head", None, None, "req"),
            P("head", "req", None),
        ),
        out_specs=P(("req", "head"), None),
        check_vma=False,
    )
```

profile of v0, /device:TPU:1, one launch (start us, length us, event | category | flops | bytes accessed | tf_op | source)
XLA Modules:
  0.0 546.9 jit_solution(2003070784256341825)
XLA Ops:
  9.7 13.4 %all-gather = s32[8,64,2]{1,2,0:T(2,128)S(1)} all-gather(s32[1,64,2]{1,2,0:T(2,128)} %bitcast.138), channel_id=1, replica_groups=mesh['req'=16,'head'=8] {'head'}, dimensions={0}, use_global_device_ids=true | all-gather | bytes 4608 | tf_op jit(solution)/shard_map/all_gather | solution.py:89
  23.4 2.3 reduce-window.6
  29.5 4.3 scatter_custom_fusion
  34.6 5.1 all-reduce.3
  41.9 3.2 concatenate.18
  45.1 15.1 %gather_fusion = bf16[1536,2048]{1,0:T(8,128)(2,1)} fusion(bf16[513,2048]{1,0:T(8,128)(2,1)} %concatenate.18, s32[2048]{0:T(1024)S(1)} %pad_clamp_fusion.1), kind=kCustom, calls=%fused_computation | custom fusion | bytes 12589056 | tf_op jit(solution)/shard_map/gather | solution.py:102
  60.1 8.1 %fusion.53 = f32[8,192,256]{2,1,0:T(8,128)} fusion(bf16[8,192,2048]{2,1,0:T(8,128)(2,1)} %bitcast.127, bf16[8,2048,256]{2,1,0:T(8,128)(2,1)} %param.20), kind=kOutput, calls=%fused_computation.131 | convolution fusion | flops 1610612736 | bytes 16252928 | tf_op jit(solution)/shard_map/ecd,edf->ecf/dot_general | solution.py:103
  68.3 6.1 %gather_fusion.1 = f32[1024,256]{1,0:T(8,128)} fusion(f32[1536,256]{1,0:T(8,128)} %bitcast.125, s32[1024]{0:T(1024)S(1)} %broadcast_clamp_fusion), kind=kCustom, calls=%fused_computation.1 | custom fusion | bytes 2101248 | tf_op jit(solution)/shard_map/gather | solution.py:104
  74.3 2.7 reshape.344
  77.1 4.5 fusion.49
  83.1 2.0 copy.132
  85.1 2.0 copy.133
  91.1 2.1 fusion.51
  96.7 5.5 %gather_fusion.2 = bf16[1536,256]{1,0:T(8,128)(2,1)} fusion(bf16[1025,256]{1,0:T(8,128)(2,1)S(1)} %concatenate.20, s32[2048]{0:T(1024)S(1)} %pad_clamp_fusion), kind=kCustom, calls=%fused_computation.2 | custom fusion | bytes 1579008 | tf_op jit(solution)/shard_map/gather | solution.py:144
  102.2 10.0 %fusion.54 = f32[8,192,2048]{2,1,0:T(8,128)} fusion(bf16[8,192,256]{2,1,0:T(8,128)(2,1)} %bitcast.128, bf16[8,256,2048]{2,1,0:T(8,128)(2,1)} %param.23), kind=kOutput, calls=%fused_computation.132 | convolution fusion | flops 1610612736 | bytes 21757952 | tf_op jit(solution)/shard_map/ecf,efd->ecd/dot_general | solution.py:145
  112.3 13.6 %gather_fusion.3 = f32[1024,2048]{1,0:T(8,128)} fusion(f32[1536,2048]{1,0:T(8,128)} %bitcast.124, s32[1024]{0:T(1024)S(1)} %broadcast_clamp_fusion), kind=kCustom, calls=%fused_computation.3 | custom fusion | bytes 16781312 | tf_op jit(solution)/shard_map/gather | solution.py:147
  125.9 10.6 %gather.32 = f32[512,2,2048]{2,1,0:T(2,128)} reshape(f32[1024,2048]{1,0:T(8,128)} %gather_fusion.3) | data formatting | bytes 16777216 | tf_op jit(solution)/shard_map/gather | solution.py:147
  136.5 3.3 fusion.55
  139.8 6.5 %gather_fusion.6 = f32[1024]{0:T(1024)S(1)} fusion(f32[512,8]{0,1:T(8,128)S(1)} %fusion.55, s32[1024]{0:T(1024)S(1)} %reshape.403), kind=kCustom, calls=%fused_computation.6 | custom fusion | bytes 16384 | tf_op jit(solution)/shard_map/jit(take_along_axis)/gather | solution.py:22
  146.9 15.1 %multiply_reduce_fusion = bf16[512,2048]{1,0:T(8,128)(2,1)} fusion(f32[512,2,2048]{2,1,0:T(2,128)} %gather.32, f32[512,2]{1,0:T(8,128)S(1)} %copy.118), kind=kLoop, calls=%fused_computation.14 | loop fusion | flops 3145728 | bytes 10489856 | tf_op jit(solution)/shard_map/reduce_sum | solution.py:149
  164.1 31.6 %reduce-scatter.3.cloned.1.call-done = bf16[64,2048]{1,0:T(8,128)(2,1)} async-done(((bf16[512,2048]{1,0:T(8,128)(2,1)}), bf16[64,2048]{1,0:T(8,128)(2,1)}) %reduce-scatter.3.cloned.1.call-update) | async-done | bytes 262160 | tf_op jit(solution)/shard_map/reduce_scatter | solution.py:150
  198.6 2.0 gather_fusion.4
  200.7 19.3 %all_to_all.10 = bf16[8,24,2048]{2,1,0:T(8,128)(2,1)S(1)} all-to-all(bf16[8,24,2048]{2,1,0:T(8,128)(2,1)} %bitcast.129), channel_id=1, replica_groups=mesh['req'=16,'head'=8] {'head'}, dimensions={0} | all-to-all | bytes 1572864 | tf_op jit(solution)/shard_map/all_to_all | solution.py:167
  221.4 89.2 %all-gather.6.cloned.1.call-done = bf16[128,24,2048]{2,0,1:T(8,128)(2,1)} async-done(((bf16[8,24,2048]{2,0,1:T(8,128)(2,1)}), bf16[128,24,2048]{2,0,1:T(8,128)(2,1)}) %all-gather.6.cloned.1.call-update) | async-done | bytes 12582928 | tf_op jit(solution)/shard_map/all_gather | solution.py:168
  310.6 12.0 %fusion.4 = f32[128,1,24,2,352]{0,4,3,2,1:T(8,128)S(1)} fusion(bf16[128,24,2048]{2,0,1:T(8,128)(2,1)} %all-gather.6.cloned.1.call-done, bf16[1,2048,2,352]{1,3,2,0:T(8,128)(2,1)S(1)} %copy-done), kind=kOutput, calls=%fused_computation.20 | convolution fusion | flops 8858370048 | bytes 24117248 | tf_op jit(solution)/shard_map/mecd,edgf->mecgf/dot_general | solution.py:171
  322.7 9.7 %convert_bitcast_fusion = bf16[128,1,24,2048]{3,0,2,1:T(8,128)(2,1)} fusion(f32[128,1,24,2,352]{0,4,3,2,1:T(8,128)S(1)} %fusion.4, bf16[1,352,2048]{2,1,0:T(8,128)(2,1)S(1)} %copy-done.14), kind=kOutput, calls=%fused_computation.13 | convolution fusion | flops 4441964544 | bytes 22675456 | tf_op jit(solution)/shard_map/mecf,efd->mecd/dot_general | solution.py:173
  334.2 176.1 %all-reduce.7.cloned.1.call-done = bf16[128,24,2048]{2,0,1:T(8,128)(2,1)} async-done(((bf16[128,24,2048]{2,0,1:T(8,128)(2,1)}), bf16[128,24,2048]{2,0,1:T(8,128)(2,1)}) %all-reduce.7.cloned.1.call-update) | async-done | bytes 12582928
  512.8 5.3 all-to-all-start.1
  519.8 10.5 %all-to-all-done.1 = bf16[8,24,2048]{2,1,0:T(8,128)(2,1)} async-done(((bf16[8,24,2048]{2,1,0:T(8,128)(2,1)}), bf16[8,24,2048]{2,1,0:T(8,128)(2,1)}, u32[]{:S(2)}, u32[]{:S(2)}) %all-to-all-start.1) | async-done | bytes 786464 | tf_op jit(solution)/shard_map/all_to_all | solution.py:185
  530.3 3.5 gather_fusion.5
  533.8 2.7 reshape.354
  536.5 2.8 multiply_reduce_fusion.1
  (129 shorter events, 31.4 us)
Async XLA Ops:
  6.5 304.1 %copy-start = (bf16[1,2048,2,352]{1,3,2,0:T(8,128)(2,1)S(1)}, bf16[1,2048,2,352]{1,3,2,0:T(8,128)(2,1)}, u32[]{:S(2)}) copy-start(bf16[1,2048,2,352]{1,3,2,0:T(8,128)(2,1)} %param.26) | copy-start | bytes 8650756
  6.5 35.3 %all-gather.4.cloned.1.call-start = ((), (), s32[]{:S(2)}) async-start(), calls=%async_computation.3 | async-start | bytes 2359296 | tf_op jit(solution)/shard_map/all_gather | solution.py:87
  9.6 186.0 %reduce-scatter.3.cloned.1.call-start = ((), (), s32[]{:S(2)}) async-start(), calls=%async_computation.4 | async-start | bytes 2359296 | tf_op jit(solution)/shard_map/reduce_scatter | solution.py:150
  26.4 0.6 copy-start.9
  77.1 4.5 copy-start.1
  77.1 4.5 copy-start.15
  88.9 2.2 copy-start.7
  91.1 2.2 copy-start.2
  91.1 2.2 copy-start.16
  125.9 10.6 %copy-start.8 = (f32[2048,8]{0,1:T(8,128)S(1)}, f32[2048,8]{0,1:T(8,128)}, u32[]{:S(2)}) copy-start(f32[2048,8]{0,1:T(8,128)} %param.19) | copy-start | bytes 196612
  139.8 6.9 %copy-start.10 = (s32[512,2]{0,1:T(2,128)S(1)}, s32[512,2]{0,1:T(2,128)}, u32[]{:S(2)}) copy-start(s32[512,2]{0,1:T(2,128)} %copy-done.9) | copy-start | bytes 12292
  146.9 15.2 %copy-start.12 = (s32[64,2]{0,1:T(2,128)S(1)}, s32[64,2]{0,1:T(2,128)}, u32[]{:S(2)}) copy-start(s32[64,2]{0,1:T(2,128)} %param.17) | copy-start | bytes 1540
  146.9 48.8 %copy-start.3 = (bf16[64,2048]{1,0:T(8,128)(2,1)S(1)}, bf16[64,2048]{1,0:T(8,128)(2,1)}, u32[]{:S(2)}) copy-start(bf16[64,2048]{1,0:T(8,128)(2,1)} %param.14) | copy-start | bytes 786436
  146.9 49.9 %copy-start.13 = (f32[2048]{0:T(1024)S(1)}, f32[2048]{0:T(1024)}, u32[]{:S(2)}) copy-start(f32[2048]{0:T(1024)} %param.24) | copy-start | bytes 24580
  162.0 148.6 %all-gather.6.cloned.1.call-start = ((), (), s32[]{:S(2)}) async-start(), calls=%async_computation.5 | async-start | bytes 13369344 | tf_op jit(solution)/shard_map/all_gather | solution.py:168
  197.9 0.7 copy-start.5
  221.3 288.9 %all-reduce.7.cloned.1.call-start = ((), (), s32[]{:S(2)}) async-start(), calls=%async_computation.6 | async-start | bytes 25165824
  310.6 12.0 %copy-start.14 = (bf16[1,352,2048]{2,1,0:T(8,128)(2,1)S(1)}, bf16[1,352,2048]{2,1,0:T(8,128)(2,1)}, u32[]{:S(2)}) copy-start(bf16[1,352,2048]{2,1,0:T(8,128)(2,1)} %param.27) | copy-start | bytes 4325380
  332.3 0.7 copy-start.17
  332.4 185.7 %copy-start.6 = (bf16[64,2048]{1,0:T(8,128)(2,1)S(1)}, bf16[64,2048]{1,0:T(8,128)(2,1)}, u32[]{:S(2)}) copy-start(bf16[64,2048]{1,0:T(8,128)(2,1)} %copy-done.5) | copy-start | bytes 786436
  332.4 185.7 %copy-start.11 = (f32[2048,8]{0,1:T(8,128)S(1)}, f32[2048,8]{0,1:T(8,128)}, u32[]{:S(2)}) copy-start(f32[2048,8]{0,1:T(8,128)} %param.25) | copy-start | bytes 196612
  512.8 17.5 %all-to-all-start.1 = ((bf16[8,24,2048]{2,1,0:T(8,128)(2,1)}), bf16[8,24,2048]{2,1,0:T(8,128)(2,1)}, u32[]{:S(2)}, u32[]{:S(2)}) async-start(bf16[8,24,2048]{2,1,0:T(8,128)(2,1)} %copy.122), calls=%async_computation.2 | async-start | bytes 1572864 | tf_op jit(solution)/shard_map/all_to_all | solution.py:185
  519.4 19.9 %copy-start.4 = (bf16[64,2048]{1,0:T(8,128)(2,1)S(1)}, bf16[64,2048]{1,0:T(8,128)(2,1)}, u32[]{:S(2)}) copy-start(bf16[64,2048]{1,0:T(8,128)(2,1)} %reduce-scatter.3.cloned.1.call-done) | copy-start | bytes 786436
Sparse Core Ops, SparseCore 0:
  9.7 29.1 all-gather.3
  162.2 33.4 reduce-scatter.2
  221.4 89.1 all-gather.5
  332.5 177.7 all-reduce.6
where the time goes:
time: 552 us; the launch traced here: 547 us
  waiting for transfers between devices  308 us (56%)
  local copies, waits for them, and re-layouts  99.4 us (18%)
  matrix products  47 us (9%)
  blocking collectives  37.8 us (7%)
  other arithmetic  34.5 us (6%)
  between operations  15.2 us (3%)
    unnamed x5, waiting for transfers between devices  176 us
    all_gather x1, waiting for transfers between devices, per_device(): shard_rows = lax.all_gather(arrived, 'req', axis=0, tiled=True)  89.2 us
    reduce_scatter x1, waiting for transfers between devices, per_device(): lax.psum_scatter(partial_value.astype(jnp.bfloat16), 'head', scatter_dime...  31.6 us
    gather x2, local copies, waits for them, and re-layouts, per_device(): projected.reshape(E_ATT * capacity, D)[slot_index]  24.2 us
    all_to_all x1, blocking collectives, per_device(): lax.all_to_all(outgoing, 'head', split_axis=0, concat_axis=0, tiled=True)  19.3 us
    reduce_sum x1, other arithmetic, per_device(): partial_value = jnp.sum(per_pair.reshape(seq_length, 2, D), axis=1)  15.1 us
    gather x1, local copies, waits for them, and re-layouts, per_device(): buffer = padded[slot_table // 2].reshape(E_ATT, capacity, D)  15.1 us
    all_gather x1, blocking collectives, per_device(): lax.all_gather(attn_routes, 'head', axis=0, tiled=True)  13.4 us
  transfers between devices with their start and end apart: 5, of which 4 were waited for; matrix products, arithmetic and copies ran while one was open for 3% of the time, Pallas kernels for 0%

commit v1 on v0

--- a/solution.py
+++ b/solution.py
@@ -165,7 +165,10 @@
     padded_ffn = jnp.concatenate([ffn_normed, jnp.zeros((1, D), jnp.bfloat16)], axis=0)
     outgoing = padded_ffn[send_table // 2].reshape(head_count, local_experts * cap_ffn, D)
     arrived = lax.all_to_all(outgoing, "head", split_axis=0, concat_axis=0, tiled=True)
-    shard_rows = lax.all_gather(arrived, "req", axis=0, tiled=True)
+    devices = lax.axis_size("req")
+    blocks = jnp.stack([arrived for _ in range(devices)])
+    blocks = lax.all_to_all(blocks, "req", split_axis=0, concat_axis=0)
+    shard_rows = jnp.concatenate(blocks, axis=0)
     row_total = shard_rows.shape[0]
     grouped = shard_rows.reshape(row_total, local_experts, cap_ffn, D)
     gate_up = jnp.einsum("mecd,edgf->mecgf", grouped, w_gate_up, preferred_element_type=jnp.float32)

time: 552 us -> 613 us (1.11)
  blocking collectives: 37.8 us -> 184 us
  waiting for transfers between devices: 308 us -> 215 us
  local copies, waits for them, and re-layouts: 99.4 us -> 107 us
    all_to_all x0 -> x1, blocking collectives: none -> 146 us  [per_device(): blocks = lax.all_to_all(blocks, 'req', split_axis=0, concat_axis=0)]
    all_gather x1 -> x0, waiting for transfers between devices: 89.2 us -> none  [per_device(): shard_rows = lax.all_gather(arrived, 'req', axis=0, tiled=True)]
    another operation x0 -> x1, local copies, waits for them, and re-layouts: none -> 7.31 us  [per_device(): blocks = jnp.stack([arrived for _ in range(devices)])]
    unnamed x5 -> x4, waiting for transfers between devices: 176 us -> 173 us
  transfers between devices with their start and end apart: 5 -> 4, of which waited for: 4 -> 3; matrix products, arithmetic and copies ran while one was open for 3% -> 3% of each run, Pallas kernels for 0% -> 0%
where the time goes in v1:
time: 613 us; the launch traced here: 608 us
  waiting for transfers between devices  215 us (35%)
  blocking collectives  184 us (30%)
  local copies, waits for them, and re-layouts  107 us (17%)
  matrix products  46 us (8%)
  other arithmetic  34.5 us (6%)
  between operations  15.3 us (2%)
    unnamed x4, waiting for transfers between devices  173 us
    all_to_all x1, blocking collectives, per_device(): blocks = lax.all_to_all(blocks, 'req', split_axis=0, concat_axis=0)  146 us
    reduce_scatter x1, waiting for transfers between devices, per_device(): lax.psum_scatter(partial_value.astype(jnp.bfloat16), 'head', scatter_dime...  31.6 us
    gather x2, local copies, waits for them, and re-layouts, per_device(): projected.reshape(E_ATT * capacity, D)[slot_index]  24.2 us
    all_to_all x1, blocking collectives, per_device(): lax.all_to_all(outgoing, 'head', split_axis=0, concat_axis=0, tiled=True)  19.3 us
    gather x1, local copies, waits for them, and re-layouts, per_device(): buffer = padded[slot_table // 2].reshape(E_ATT, capacity, D)  15.1 us
    reduce_sum x1, other arithmetic, per_device(): partial_value = jnp.sum(per_pair.reshape(seq_length, 2, D), axis=1)  15.1 us
    all_gather x1, blocking collectives, per_device(): lax.all_gather(attn_routes, 'head', axis=0, tiled=True)  13.4 us
  transfers between devices with their start and end apart: 4, of which 3 were waited for; matrix products, arithmetic and copies ran while one was open for 3% of the time, Pallas kernels for 0%

profile of v1, /device:TPU:1, one launch (start us, length us, event | category | flops | bytes accessed | tf_op | source)
XLA Modules:
  0.0 607.6 jit_solution(16110153669978228963)
XLA Ops:
  9.7 13.4 %all-gather = s32[8,64,2]{1,2,0:T(2,128)S(1)} all-gather(s32[1,64,2]{1,2,0:T(2,128)} %bitcast.140), channel_id=1, replica_groups=mesh['req'=16,'head'=8] {'head'}, dimensions={0}, use_global_device_ids=true | all-gather | bytes 4608 | tf_op jit(solution)/shard_map/all_gather | solution.py:89
  23.4 2.3 reduce-window.6
  29.5 4.3 scatter_custom_fusion
  34.6 5.1 all-reduce.3
  41.9 3.2 concatenate.18
  45.1 15.1 %gather_fusion = bf16[1536,2048]{1,0:T(8,128)(2,1)} fusion(bf16[513,2048]{1,0:T(8,128)(2,1)} %concatenate.18, s32[2048]{0:T(1024)S(1)} %pad_clamp_fusion.1), kind=kCustom, calls=%fused_computation | custom fusion | bytes 12589056 | tf_op jit(solution)/shard_map/gather | solution.py:102
  60.2 8.1 %fusion.54 = f32[8,192,256]{2,1,0:T(8,128)} fusion(bf16[8,192,2048]{2,1,0:T(8,128)(2,1)} %bitcast.129, bf16[8,2048,256]{2,1,0:T(8,128)(2,1)} %param.20), kind=kOutput, calls=%fused_computation.132 | convolution fusion | flops 1610612736 | bytes 16252928 | tf_op jit(solution)/shard_map/ecd,edf->ecf/dot_general | solution.py:103
  68.3 6.1 gather_fusion.1
  74.4 2.7 reshape.347
  77.1 4.3 fusion.50
  81.5 2.6 fusion.53
  92.9 2.1 fusion.52
  98.5 5.5 gather_fusion.2
  104.0 10.0 %fusion.55 = f32[8,192,2048]{2,1,0:T(8,128)} fusion(bf16[8,192,256]{2,1,0:T(8,128)(2,1)} %bitcast.130, bf16[8,256,2048]{2,1,0:T(8,128)(2,1)} %param.23), kind=kOutput, calls=%fused_computation.133 | convolution fusion | flops 1610612736 | bytes 21757952 | tf_op jit(solution)/shard_map/ecf,efd->ecd/dot_general | solution.py:145
  114.0 13.6 %gather_fusion.3 = f32[1024,2048]{1,0:T(8,128)} fusion(f32[1536,2048]{1,0:T(8,128)} %bitcast.126, s32[1024]{0:T(1024)S(1)} %broadcast_clamp_fusion), kind=kCustom, calls=%fused_computation.3 | custom fusion | bytes 16781312 | tf_op jit(solution)/shard_map/gather | solution.py:147
  127.7 10.6 %gather.32 = f32[512,2,2048]{2,1,0:T(2,128)} reshape(f32[1024,2048]{1,0:T(8,128)} %gather_fusion.3) | data formatting | bytes 16777216 | tf_op jit(solution)/shard_map/gather | solution.py:147
  138.3 3.3 fusion.56
  141.6 6.5 %gather_fusion.6 = f32[1024]{0:T(1024)S(1)} fusion(f32[512,8]{0,1:T(8,128)S(1)} %fusion.56, s32[1024]{0:T(1024)S(1)} %reshape.407), kind=kCustom, calls=%fused_computation.6 | custom fusion | bytes 16384 | tf_op jit(solution)/shard_map/jit(take_along_axis)/gather | solution.py:22
  148.7 15.1 %multiply_reduce_fusion = bf16[512,2048]{1,0:T(8,128)(2,1)} fusion(f32[512,2,2048]{2,1,0:T(2,128)} %gather.32, f32[512,2]{1,0:T(8,128)S(1)} %copy.121), kind=kLoop, calls=%fused_computation.15 | loop fusion | flops 3145728 | bytes 10489856 | tf_op jit(solution)/shard_map/reduce_sum | solution.py:149
  165.8 31.6 %reduce-scatter.3.cloned.1.call-done = bf16[64,2048]{1,0:T(8,128)(2,1)} async-done(((bf16[512,2048]{1,0:T(8,128)(2,1)}), bf16[64,2048]{1,0:T(8,128)(2,1)}) %reduce-scatter.3.cloned.1.call-update) | async-done | bytes 262160 | tf_op jit(solution)/shard_map/reduce_scatter | solution.py:150
  200.4 2.0 gather_fusion.4
  202.4 19.3 %all_to_all.15 = bf16[8,24,2048]{2,1,0:T(8,128)(2,1)S(1)} all-to-all(bf16[8,24,2048]{2,1,0:T(8,128)(2,1)} %bitcast.131), channel_id=1, replica_groups=mesh['req'=16,'head'=8] {'head'}, dimensions={0} | all-to-all | bytes 1572864 | tf_op jit(solution)/shard_map/all_to_all | solution.py:167
  223.1 7.3 %stack.7 = bf16[16,8,24,2048]{3,1,2,0:T(8,128)(2,1)} broadcast(bf16[8,24,2048]{2,0,1:T(8,128)(2,1)} %copy.124), dimensions={1,2,3} | broadcast | bytes 13369344 | tf_op jit(solution)/shard_map/stack | solution.py:169
  230.4 146.3 %all_to_all.16 = bf16[16,8,24,2048]{3,1,2,0:T(8,128)(2,1)S(1)} all-to-all(bf16[16,8,24,2048]{3,1,2,0:T(8,128)(2,1)} %stack.7), channel_id=1, replica_groups=mesh['req'=16,'head'=8] {'req'}, dimensions={0} | all-to-all | bytes 25165824 | tf_op jit(solution)/shard_map/all_to_all | solution.py:170
  376.7 9.1 %fusion.5 = f32[128,1,24,2,352]{0,4,3,2,1:T(8,128)S(1)} fusion(bf16[16,8,24,2048]{3,1,2,0:T(8,128)(2,1)S(1)} %all_to_all.16, bf16[1,2048,2,352]{1,3,2,0:T(8,128)(2,1)S(1)} %copy-done), kind=kOutput, calls=%fused_computation.21 | convolution fusion | flops 8858370048 | bytes 24117248 | tf_op jit(solution)/shard_map/mecd,edgf->mecgf/dot_general | solution.py:174
  385.9 9.7 %convert_bitcast_fusion = bf16[128,1,24,2048]{3,0,2,1:T(8,128)(2,1)} fusion(f32[128,1,24,2,352]{0,4,3,2,1:T(8,128)S(1)} %fusion.5, bf16[1,352,2048]{2,1,0:T(8,128)(2,1)S(1)} %copy-done.13), kind=kOutput, calls=%fused_computation.14 | convolution fusion | flops 4441964544 | bytes 22675456 | tf_op jit(solution)/shard_map/mecf,efd->mecd/dot_general | solution.py:176
  397.4 173.3 %all-reduce.7.cloned.1.call-done = bf16[128,24,2048]{2,0,1:T(8,128)(2,1)} async-done(((bf16[128,24,2048]{2,0,1:T(8,128)(2,1)}), bf16[128,24,2048]{2,0,1:T(8,128)(2,1)}) %all-reduce.7.cloned.1.call-update) | async-done | bytes 12582928
  573.3 5.6 all-to-all-start.2
  580.6 10.5 %all-to-all-done.2 = bf16[8,24,2048]{2,1,0:T(8,128)(2,1)} async-done(((bf16[8,24,2048]{2,1,0:T(8,128)(2,1)}), bf16[8,24,2048]{2,1,0:T(8,128)(2,1)}, u32[]{:S(2)}, u32[]{:S(2)}) %all-to-all-start.2) | async-done | bytes 786464 | tf_op jit(solution)/shard_map/all_to_all | solution.py:188
  591.0 3.5 gather_fusion.5
  594.5 2.7 reshape.358
  597.2 2.8 multiply_reduce_fusion.1
  (124 shorter events, 34.5 us)
Async XLA Ops:
  6.5 370.2 %copy-start = (bf16[1,2048,2,352]{1,3,2,0:T(8,128)(2,1)S(1)}, bf16[1,2048,2,352]{1,3,2,0:T(8,128)(2,1)}, u32[]{:S(2)}) copy-start(bf16[1,2048,2,352]{1,3,2,0:T(8,128)(2,1)} %param.26) | copy-start | bytes 8650756
  6.5 35.3 %all-gather.3.cloned.1.call-start = ((), (), s32[]{:S(2)}) async-start(), calls=%async_computation.4 | async-start | bytes 2359296 | tf_op jit(solution)/shard_map/all_gather | solution.py:87
  9.6 187.8 %reduce-scatter.3.cloned.1.call-start = ((), (), s32[]{:S(2)}) async-start(), calls=%async_computation.5 | async-start | bytes 2359296 | tf_op jit(solution)/shard_map/reduce_scatter | solution.py:150
  26.4 0.6 copy-start.8
  90.6 2.2 copy-start.6
  92.9 2.2 copy-start.1
  92.9 2.2 copy-start.14
  127.7 10.6 %copy-start.7 = (f32[2048,8]{0,1:T(8,128)S(1)}, f32[2048,8]{0,1:T(8,128)}, u32[]{:S(2)}) copy-start(f32[2048,8]{0,1:T(8,128)} %param.19) | copy-start | bytes 196612
  141.6 6.9 %copy-start.9 = (s32[512,2]{0,1:T(2,128)S(1)}, s32[512,2]{0,1:T(2,128)}, u32[]{:S(2)}) copy-start(s32[512,2]{0,1:T(2,128)} %copy-done.8) | copy-start | bytes 12292
  148.6 15.2 %copy-start.11 = (s32[64,2]{0,1:T(2,128)S(1)}, s32[64,2]{0,1:T(2,128)}, u32[]{:S(2)}) copy-start(s32[64,2]{0,1:T(2,128)} %param.17) | copy-start | bytes 1540
  148.7 48.8 %copy-start.2 = (bf16[64,2048]{1,0:T(8,128)(2,1)S(1)}, bf16[64,2048]{1,0:T(8,128)(2,1)}, u32[]{:S(2)}) copy-start(bf16[64,2048]{1,0:T(8,128)(2,1)} %param.14) | copy-start | bytes 786436
  148.7 49.9 %copy-start.12 = (f32[2048]{0:T(1024)S(1)}, f32[2048]{0:T(1024)}, u32[]{:S(2)}) copy-start(f32[2048]{0:T(1024)} %param.24) | copy-start | bytes 24580
  163.8 406.9 %all-reduce.7.cloned.1.call-start = ((), (), s32[]{:S(2)}) async-start(), calls=%async_computation.6 | async-start | bytes 25165824
  199.7 0.7 copy-start.4
  376.7 9.2 %copy-start.13 = (bf16[1,352,2048]{2,1,0:T(8,128)(2,1)S(1)}, bf16[1,352,2048]{2,1,0:T(8,128)(2,1)}, u32[]{:S(2)}) copy-start(bf16[1,352,2048]{2,1,0:T(8,128)(2,1)} %param.27) | copy-start | bytes 4325380
  395.6 0.7 copy-start.15
  395.6 183.2 %copy-start.5 = (bf16[64,2048]{1,0:T(8,128)(2,1)S(1)}, bf16[64,2048]{1,0:T(8,128)(2,1)}, u32[]{:S(2)}) copy-start(bf16[64,2048]{1,0:T(8,128)(2,1)} %copy-done.4) | copy-start | bytes 786436
  395.6 183.2 %copy-start.10 = (f32[2048,8]{0,1:T(8,128)S(1)}, f32[2048,8]{0,1:T(8,128)}, u32[]{:S(2)}) copy-start(f32[2048,8]{0,1:T(8,128)} %param.25) | copy-start | bytes 196612
  573.3 17.8 %all-to-all-start.2 = ((bf16[8,24,2048]{2,1,0:T(8,128)(2,1)}), bf16[8,24,2048]{2,1,0:T(8,128)(2,1)}, u32[]{:S(2)}, u32[]{:S(2)}) async-start(bf16[8,24,2048]{2,1,0:T(8,128)(2,1)} %copy.126), calls=%async_computation.3 | async-start | bytes 1572864 | tf_op jit(solution)/shard_map/all_to_all | solution.py:188
  580.2 19.8 %copy-start.3 = (bf16[64,2048]{1,0:T(8,128)(2,1)S(1)}, bf16[64,2048]{1,0:T(8,128)(2,1)}, u32[]{:S(2)}) copy-start(bf16[64,2048]{1,0:T(8,128)(2,1)} %reduce-scatter.3.cloned.1.call-done) | copy-start | bytes 786436
Sparse Core Ops, SparseCore 0:
  9.7 29.1 all-gather.2
  163.9 33.4 reduce-scatter.2
  395.7 174.9 all-reduce.6
